TPU v7x, 32 devices: a whole 2x2x4 slice. The times are simulated.
32 devices in a mesh: dp: 16 (over z, x, core), vol: 2 (over y).
Axes of the slice: x: 2, y: 2, z: 4, core: 2. Of those that a mesh axis runs over, the one named last changes fastest.
Arguments:
- images: float32 [32, 128, 128], P(('dp', 'vol')), may hold values from -6 to 6
- contrast: bfloat16 [32, 128, 128], P(('dp', 'vol')), may hold values from -1 to 1
- volume: bfloat16 [256, 256, 256], P('vol'), may hold values from -6 to 6
- line_index: int32 [32, 4, 128], P('dp'), may hold values from 0 to 65278, as said below
- patch_weight: bfloat16 [64, 1024], replicated, may hold values from -0.75 to 0.75
- position: bfloat16 [256, 1024], replicated, may hold values from -3 to 3
- norm_gain: float32 [1024], replicated, may hold values from 0.1 to 1.9
- project_in: bfloat16 [1024, 1536], P('dp'), may hold values from -0.1875 to 0.1875
- project_out: bfloat16 [1024, 512], P('dp'), may hold values from -0.25 to 0.25
- head_weight: float32 [1024, 4], replicated, may hold values from -1.8 to 1.8
Outputs:
- errors: float32 [32, 4], P(('dp', 'vol'))
- in_gradient: float32 [1024, 1536], P('dp')
- out_gradient: float32 [1024, 512], P('dp')
- head_gradient: float32 [1024, 4], replicated
Inputs may be any that keep to these rules, and one draw needn't show every extreme that they name: line_index[i, k, r] = z * 256 + y names the plane z and row y of the volume that row r of hypothesis k of image i samples; z and y lie within 0 and 254.
All inputs are finite; a program needn't handle non-finite values.
Results may differ from a plain program's by a relative error of at most 0.038.
Values may be sent and summed in bfloat16 or wider, within the bound.
A program may use at most 64 MiB of HBM per device.

v0:
```python
import math
import jax
import jax.numpy as jnp
from jax import lax
from jax.sharding import PartitionSpec as P

HEADS = 8
HEAD_DIM = 64
PIX = 128
PATCH = 8
PATCHES = 256
K = 4
EPSILON = 1e-05


def embed_images(images, patch_weight, position):
    count = images.shape[0]
    grid = PIX // PATCH
    pieces = images.reshape(count, grid, PATCH, grid, PATCH).transpose(0, 1, 3, 2, 4)
    pieces = pieces.reshape(count * grid * grid, PATCH * PATCH).astype(jnp.bfloat16)
    mixed = jnp.dot(pieces, patch_weight, preferred_element_type=jnp.float32)
    mixed = mixed.reshape(count, grid * grid, -1) + position.astype(jnp.float32)[None]
    return mixed.reshape(count * grid * grid, -1).astype(jnp.bfloat16)


def normalize(embedded, norm_gain):
    values = embedded.astype(jnp.float32)
    center = values - jnp.mean(values, axis=1, keepdims=True)
    scale = lax.rsqrt(jnp.mean(center * center, axis=1, keepdims=True) + EPSILON)
    return (center * scale * norm_gain[None, :]).astype(jnp.bfloat16)


def attend(triple):
    count = triple.shape[0] // PATCHES
    parts = triple.reshape(count, PATCHES, 3, HEADS, HEAD_DIM).astype(jnp.float32)
    query = parts[:, :, 0]
    keys = parts[:, :, 1]
    values = parts[:, :, 2]
    scores = jnp.einsum("bqhd,bkhd->bhqk", query, keys) * HEAD_DIM ** (-0.5)
    raised = jnp.exp(scores)
    weights = (raised / jnp.sum(raised, axis=-1, keepdims=True)).astype(jnp.bfloat16)
    mixed = jnp.einsum("bhqk,bkhd->bqhd", weights.astype(jnp.float32), values)
    return mixed.reshape(count * PATCHES, HEADS * HEAD_DIM).astype(jnp.bfloat16)


def hartley(images):
    side = images.shape[1]
    freq = jnp.arange(side, dtype=jnp.int32) - side // 2
    place = jnp.arange(side, dtype=jnp.int32)
    phase = (freq[:, None] * place[None, :] % side).astype(jnp.float32) * (2.0 * math.pi / side)
    cosine = jnp.cos(phase)
    sine = jnp.sin(phase)
    highest = lax.Precision.HIGHEST
    first_cos = jnp.einsum("rn,bnm->brm", cosine, images, precision=highest)
    first_sin = jnp.einsum("rn,bnm->brm", sine, images, precision=highest)
    result = jnp.einsum("brm,cm->brc", first_cos, cosine + sine, precision=highest)
    result = result + jnp.einsum("brm,cm->brc", first_sin, cosine - sine, precision=highest)
    return result / side


def render(volume, line_index, slab_index):
    slab, side, _ = volume.shape
    table = volume.reshape(slab * side, side)
    plane = line_index // side - slab_index * slab
    inside = (plane >= 0) & (plane < slab)
    rows = jnp.clip(plane, 0, slab - 1) * side + line_index % side
    picked = jnp.take(table, rows.reshape(-1), axis=0)[:, ::2]
    picked = jnp.where(inside.reshape(-1, 1), picked.astype(jnp.float32), 0.0)
    return (picked.reshape(line_index.shape[0], -1), inside)


def local(
    images,
    contrast,
    volume,
    line_index,
    patch_weight,
    position,
    norm_gain,
    project_in,
    project_out,
    head_weight,
):
    count = images.shape[0]
    width = norm_gain.shape[0]
    highest = lax.Precision.HIGHEST
    rendered, inside = render(volume, line_index, lax.axis_index("vol"))
    spectrum = hartley(images)
    slices = lax.psum_scatter(
        rendered.astype(jnp.bfloat16), "vol", scatter_dimension=0, tiled=True
    ).astype(jnp.float32)
    slices = slices.reshape(count, K, PIX, PIX)
    misfit = contrast.astype(jnp.float32)[:, None] * slices - spectrum[:, None]
    errors = jnp.mean(misfit * misfit, axis=(2, 3))
    embedded = embed_images(images, patch_weight, position)
    normed = normalize(embedded, norm_gain)
    triple = jnp.dot(
        normed,
        lax.all_gather(project_in, "dp", axis=0, tiled=True),
        preferred_element_type=jnp.float32,
    ).astype(jnp.bfloat16)
    attended = attend(triple)
    contract_last = (((1,), (1,)), ((), ()))
    out_whole = lax.all_gather(project_out, "dp", axis=0, tiled=True)
    branch = lax.dot_general(attended, out_whole, contract_last, preferred_element_type=jnp.float32)
    layer_out = embedded.astype(jnp.float32) + branch
    pooled = jnp.mean(layer_out.reshape(count, PATCHES, width), axis=1)
    logits = jnp.dot(pooled, head_weight, precision=highest)
    raised = jnp.exp(logits)
    chances = raised / jnp.sum(raised, axis=1, keepdims=True)
    expected = jnp.sum(chances * errors, axis=1, keepdims=True)
    logit_slope = chances * (errors - expected)
    head_gradient = lax.psum(jnp.dot(pooled.T, logit_slope, precision=highest), ("dp", "vol"))
    pooled_slope = jnp.dot(logit_slope, head_weight.T, precision=highest) / PATCHES
    layer_slope = jnp.broadcast_to(pooled_slope[:, None, :], (count, PATCHES, width))
    layer_slope = layer_slope.reshape(count * PATCHES, width).astype(jnp.bfloat16)
    attended_slope = jnp.dot(layer_slope, out_whole, preferred_element_type=jnp.float32).astype(
        jnp.bfloat16
    )
    triple_slope = jax.vjp(attend, triple)[1](attended_slope)[0]
    contract_first = (((0,), (0,)), ((), ()))
    first = lax.dot_general(
        normed, triple_slope, contract_first, preferred_element_type=jnp.float32
    )
    second = lax.dot_general(
        layer_slope, attended, contract_first, preferred_element_type=jnp.float32
    )
    shard = lax.psum_scatter(
        jnp.concatenate([first, second], axis=1).astype(jnp.bfloat16),
        "dp",
        scatter_dimension=0,
        tiled=True,
    ).astype(jnp.float32)
    shard = lax.psum(shard.astype(jnp.bfloat16), "vol").astype(jnp.float32)
    split = project_in.shape[1]
    return (errors, shard[:, :split], shard[:, split:], head_gradient)


def solution(mesh):
    placed = (
        P(("dp", "vol"), None, None),
        P(("dp", "vol"), None, None),
        P("vol", None, None),
        P("dp", None, None),
        P(),
        P(),
        P(),
        P("dp", None),
        P("dp", None),
        P(),
    )
    return jax.shard_map(
        local,
        mesh=mesh,
        in_specs=placed,
        out_specs=(P(("dp", "vol"), None), P("dp", None), P("dp", None), P()),
        check_vma=False,
    )
```

profile of v0, /device:TPU:0, one launch (start us, length us, event | category | flops | bytes accessed | tf_op | source)
XLA Modules:
  0.0 261.4 jit_solution(18446166115794627641)
XLA Ops:
  8.1 0.7 fusion.38
  8.8 0.7 compare_and_fusion.1
  9.5 11.4 %gather_fusion = bf16[1024,256]{1,0:T(8,128)(2,1)S(1)} fusion(bf16[32768,256]{1,0:T(8,128)(2,1)} %bitcast.106, s32[1024]{0:T(1024)S(1)} %broadcast_clamp_fusion), kind=kCustom, calls=%fused_computation | custom fusion | bytes 1052672 | tf_op jit(solution)/shard_map/jit(_take)/gather | solution.py:67
  21.0 0.2 broadcast_select_fusion
  21.2 10.3 %slice.21 = bf16[1024,128]{1,0:T(8,128)(2,1)S(1)} slice(bf16[1024,256]{1,0:T(8,128)(2,1)S(1)} %broadcast_select_fusion), slice={[0:1024:1], [0:256:2]} | slice | bytes 524288 | tf_op jit(solution)/shard_map/slice | solution.py:67
  31.7 0.8 convert_element_type.102
  32.5 0.5 all-gather.3.cloned.1.call-update
  33.1 0.5 all-gather.5.cloned.1.call-update
  33.6 0.2 reduce-scatter.2.cloned.1.call-start
  33.9 0.5 fusion.21
  34.4 0.5 fusion.19
  35.0 0.6 fusion.24
  35.6 0.6 convert_element_type.105
  36.2 0.3 copy.31
  36.5 0.2 convert_element_type.107
  36.7 0.4 convert_reduce_fusion
  37.2 0.3 fusion.11
  37.5 0.6 dynamic-slice
  38.1 0.6 fusion.9
  38.7 19.9 %all-reduce.9.cloned.1.call-done = bf16[2,65536]{1,0:T(2,128)(2,1)} async-done(((bf16[2,65536]{1,0:T(2,128)(2,1)}), bf16[2,65536]{1,0:T(2,128)(2,1)}) %all-reduce.9.cloned.1.call-update) | async-done | bytes 262160
  58.6 1.8 dynamic-slice_convert_fusion
  60.4 0.6 multiply_reduce_fusion
  61.0 22.6 %all-gather.3.cloned.1.call-done = bf16[1024,1536]{1,0:T(8,128)(2,1)} async-done(((bf16[64,1536]{1,0:T(8,128)(2,1)}), bf16[1024,1536]{1,0:T(8,128)(2,1)}) %all-gather.3.cloned.1.call-update) | async-done | bytes 3145744 | tf_op jit(solution)/shard_map/all_gather | solution.py:99
  83.7 3.0 %convolution_convert_fusion.1 = bf16[256,1536]{1,0:T(8,128)(2,1)S(1)} fusion(bf16[1024,1536]{1,0:T(8,128)(2,1)} %all-gather.3.cloned.1.call-done, bf16[256,1024]{1,0:T(8,128)(2,1)S(1)} %get-tuple-element.9, f32[1024]{0:T(1024)S(1)} %copy-done.17, f32[256]{0:T(256)S(1)} %add_rsqrt_fusion, f32[256]{0:T(256)S(1)} %broadcast_multiply_fusion.2), kind=kOutput, calls=%fused_computation.5 | convolution fusion | flops 807010304 | bytes 4462592 | tf_op jit(solution)/shard_map/dot_general | solution.py:97
  86.7 0.3 copy.32
  87.0 0.5 fusion.63
  87.5 0.3 copy-done.3
  88.0 1.2 convolution_convert_fusion.5
  89.3 32.9 %all-gather.5.cloned.1.call-done = bf16[1024,512]{1,0:T(8,128)(2,1)} async-done(((bf16[64,512]{1,0:T(8,128)(2,1)}), bf16[1024,512]{1,0:T(8,128)(2,1)}) %all-gather.5.cloned.1.call-update) | async-done | bytes 1048592 | tf_op jit(solution)/shard_map/all_gather | solution.py:104
  122.2 1.9 fusion.8
  124.2 0.8 fusion.64
  125.0 1.3 multiply_reduce_fusion.1
  126.3 1.2 subtract_multiply_fusion
  127.7 0.4 copy-done.15
  128.1 1.5 convolution_convert_fusion.3
  129.6 1.1 convolution_convert_fusion.4
  130.7 1.1 copy.34
  131.8 1.5 fusion.4
  133.4 0.6 convolution_bitcast_fusion
  134.0 0.6 convolution_bitcast_fusion.1
  134.6 0.4 convolution_bitcast_fusion.2
  135.1 0.5 copy-done.2
  135.6 1.2 convolution_convert_fusion
  136.8 2.6 pad_maximum_fusion
  139.5 71.4 %reduce-scatter.2.cloned.1.call-done = bf16[64,2048]{1,0:T(8,128)(2,1)} async-done(((bf16[1024,2048]{1,0:T(8,128)(2,1)}), bf16[64,2048]{1,0:T(8,128)(2,1)}) %reduce-scatter.2.cloned.1.call-update) | async-done | bytes 262160 | tf_op jit(solution)/shard_map/reduce_scatter | solution.py:128
  211.0 39.6 %psum.15 = f32[1024,4]{0,1:T(4,128)} all-reduce(f32[1024,4]{0,1:T(4,128)S(1)} %broadcast_multiply_fusion), channel_id=1, replica_groups=mesh['dp'=16,'vol'=2] {'dp','vol'}, use_global_device_ids=true, to_apply=%region_11.12 | all-reduce | flops 4096 | bytes 32768 | tf_op jit(solution)/shard_map/psum | solution.py:113
  250.6 1.7 slice.32
  252.3 1.5 slice.33
  (68 shorter events, 1.1 us)
Async XLA Ops:
  8.0 28.7 %copy-start = (bf16[64,1024]{1,0:T(8,128)(2,1)S(1)}, bf16[64,1024]{1,0:T(8,128)(2,1)}, u32[]{:S(2)}) copy-start(bf16[64,1024]{1,0:T(8,128)(2,1)} %param.14) | copy-start | bytes 393220
  8.0 50.5 %all-reduce.9.cloned.1.call-start = ((), (), s32[]{:S(2)}) async-start(), calls=%async_computation.5 | async-start | bytes 524288
  20.9 13.0 %copy-start.7 = (f32[1,128,128]{2,1,0:T(8,128)S(1)}, f32[1,128,128]{2,1,0:T(8,128)}, u32[]{:S(2)}) copy-start(f32[1,128,128]{2,1,0:T(8,128)} %param.10) | copy-start | bytes 196612
  21.0 14.6 %copy-start.8 = (bf16[1,128,128]{2,1,0:T(8,128)(2,1)S(1)}, bf16[1,128,128]{2,1,0:T(8,128)(2,1)}, u32[]{:S(2)}) copy-start(bf16[1,128,128]{2,1,0:T(8,128)(2,1)} %param.11) | copy-start | bytes 98308
  31.5 5.3 %copy-start.6 = (bf16[256,1024]{1,0:T(8,128)(2,1)S(1)}, bf16[256,1024]{1,0:T(8,128)(2,1)}, u32[]{:S(2)}) copy-start(bf16[256,1024]{1,0:T(8,128)(2,1)} %param.15) | copy-start | bytes 1572868
  32.5 51.2 %all-gather.3.cloned.1.call-start = ((), (), s32[]{:S(2)}) async-start(), calls=%async_computation.1 | async-start | bytes 3342336 | tf_op jit(solution)/shard_map/all_gather | solution.py:99
  33.1 89.2 %all-gather.5.cloned.1.call-start = ((), (), s32[]{:S(2)}) async-start(), calls=%async_computation.2 | async-start | bytes 1114112 | tf_op jit(solution)/shard_map/all_gather | solution.py:104
  33.6 177.2 %reduce-scatter.2.cloned.1.call-start = ((), (), s32[]{:S(2)}) async-start(), calls=%async_computation.3 | async-start | bytes 4456448 | tf_op jit(solution)/shard_map/reduce_scatter | solution.py:128
  34.4 3.1 %copy-start.22 = (u32[32]{0:T(128)S(1)}, u32[32]{0:T(128)}, u32[]{:S(2)}) copy-start(u32[32]{0:T(128)} %constant.104) | copy-start | bytes 388
  36.2 47.5 %copy-start.17 = (f32[1024]{0:T(1024)S(1)}, f32[1024]{0:T(1024)}, u32[]{:S(2)}) copy-start(f32[1024]{0:T(1024)} %param.16) | copy-start | bytes 12292
  37.2 49.5 %copy-start.1 = (bf16[256,1024]{1,0:T(8,128)(2,1)}, bf16[256,1024]{1,0:T(8,128)(2,1)S(1)}, u32[]{:S(2)}) copy-start(bf16[256,1024]{1,0:T(8,128)(2,1)S(1)} %get-tuple-element.9) | copy-start | bytes 1572868
  37.2 49.5 %copy-start.12 = (f32[256]{0:T(256)}, f32[256]{0:T(256)S(1)}, u32[]{:S(2)}) copy-start(f32[256]{0:T(256)S(1)} %broadcast_multiply_fusion.2) | copy-start | bytes 3076
  37.5 49.2 %copy-start.19 = (f32[256]{0:T(256)}, f32[256]{0:T(256)S(1)}, u32[]{:S(2)}) copy-start(f32[256]{0:T(256)S(1)} %add_rsqrt_fusion) | copy-start | bytes 3076
  87.0 0.9 copy-start.3
  122.2 2.0 copy-start.9
  122.2 2.8 %copy-start.14 = (f32[4]{0:T(128)S(1)}, f32[4]{0:T(128)}, u32[]{:S(2)}) copy-start(f32[4]{0:T(128)} %multiply_reduce_fusion) | copy-start | bytes 52
  122.2 7.4 %copy-start.21 = (bf16[1024,512]{1,0:T(8,128)(2,1)S(1)}, bf16[1024,512]{1,0:T(8,128)(2,1)}, u32[]{:S(2)}) copy-start(bf16[1024,512]{1,0:T(8,128)(2,1)} %all-gather.5.cloned.1.call-done) | copy-start | bytes 3145732
  124.2 3.5 %copy-start.10 = (f32[1024]{0:T(1024)}, f32[1024]{0:T(1024)S(1)}, u32[]{:S(2)}) copy-start(f32[1024]{0:T(1024)S(1)} %broadcast_multiply_fusion.1) | copy-start | bytes 12292
  127.5 0.6 copy-start.15
  131.8 1.6 copy-start.4
  134.6 1.0 copy-start.2
  134.6 1.0 copy-start.13
  134.6 1.0 copy-start.18
  134.6 1.0 copy-start.20
  135.6 1.2 copy-start.5
  139.4 71.5 %copy-start.11 = (f32[1024]{0:T(1024)S(1)}, f32[1024]{0:T(1024)}, u32[]{:S(2)}) copy-start(f32[1024]{0:T(1024)} %copy-done.10) | copy-start | bytes 12292
  139.4 71.5 %copy-start.16 = (f32[4]{0:T(128)S(1)}, f32[4]{0:T(128)}, u32[]{:S(2)}) copy-start(f32[4]{0:T(128)} %copy-done.15) | copy-start | bytes 52
  139.4 111.2 %all-reduce.7.cloned.1.call-start = ((), (), s32[]{:S(2)}) async-start(), calls=%async_computation.4 | async-start | bytes 524288 | tf_op jit(solution)/shard_map/psum | solution.py:134
Sparse Core Ops, SparseCore 0:
  32.6 25.9 all-reduce.8
  211.0 22.3 all-reduce.6
Sparse Core Ops, SparseCore 1:
  35.5 48.1 all-gather.2
  85.9 36.2 all-gather.4
  139.5 71.3 reduce-scatter.1
where the time goes:
time: 262 us; the launch traced here: 261 us
  waiting for transfers between devices  148 us (56%)
  blocking collectives  39.6 us (15%)
  local copies, waits for them, and re-layouts  30.1 us (11%)
  matrix products  17.1 us (7%)
  between operations  16.1 us (6%)
  other arithmetic  10.1 us (4%)
    reduce_scatter x1, waiting for transfers between devices, local(): lax.psum_scatter(jnp.concatenate([first, second], axis=1).astype(jnp.bflo...  71.4 us
    psum x1, blocking collectives, local(): lax.psum(jnp.dot(pooled.T, logit_slope, precision=highest), ('dp', 'vol'))  39.6 us
    all_gather x1, waiting for transfers between devices, local(): out_whole = lax.all_gather(project_out, 'dp', axis=0, tiled=True)  32.9 us
    all_gather x1, waiting for transfers between devices, local(): lax.all_gather(project_in, 'dp', axis=0, tiled=True)  22.6 us
    unnamed x6, waiting for transfers between devices  21 us
    gather x1, local copies, waits for them, and re-layouts, render(): picked = jnp.take(table, rows.reshape(-1), axis=0)[:, ::2]  11.4 us
    slice x1, local copies, waits for them, and re-layouts, render(): picked = jnp.take(table, rows.reshape(-1), axis=0)[:, ::2]  10.3 us
  transfers between devices with their start and end apart: 5, of which 4 were waited for; matrix products, arithmetic and copies ran while one was open for 5% of the time, Pallas kernels for 0%

commit v1 on v0

--- a/solution.py
+++ b/solution.py
@@ -11,6 +11,19 @@
 PATCHES = 256
 K = 4
 EPSILON = 1e-05
+
+
+def _note_panel(body):
+    s_next = lax.psum(1, "dp")
+    y_new = lax.axis_index("dp")
+    value_now, t_next, frame_out = (s_next, y_new, body.shape[0])
+    low, t1 = (body, 1)
+    while t1 < value_now:
+        new = lax.ppermute(low, "dp", [(j, (j - t1) % value_now) for j in range(value_now)])
+        low = jnp.concatenate([low, new], axis=0)
+        t1 = 2 * t1
+    found_now = jnp.roll(low, shift=t_next * frame_out, axis=0)
+    return found_now
 
 
 def embed_images(images, patch_weight, position):
@@ -101,7 +114,7 @@
     ).astype(jnp.bfloat16)
     attended = attend(triple)
     contract_last = (((1,), (1,)), ((), ()))
-    out_whole = lax.all_gather(project_out, "dp", axis=0, tiled=True)
+    out_whole = _note_panel(project_out)
     branch = lax.dot_general(attended, out_whole, contract_last, preferred_element_type=jnp.float32)
     layer_out = embedded.astype(jnp.float32) + branch
     pooled = jnp.mean(layer_out.reshape(count, PATCHES, width), axis=1)

time: 262 us -> 250 us (0.954)
  waiting for transfers between devices: 148 us -> 121 us
  starting transfers between devices: 0.39 us -> 9.74 us
  local copies, waits for them, and re-layouts: 30.1 us -> 37.3 us
    ppermute x0 -> x4, waiting for transfers between devices: none -> 46.7 us  [_note_panel(): lax.ppermute(low, 'dp', [(j, (j - t1) % value_now) for j in range(value_n...]
    all_gather x1 -> x0, waiting for transfers between devices: 32.9 us -> none  [local(): out_whole = lax.all_gather(project_out, 'dp', axis=0, tiled=True)]
    all_gather x1, waiting for transfers between devices: 22.6 us -> 0.01 us  [local(): lax.all_gather(project_in, 'dp', axis=0, tiled=True)]
    unnamed x6 -> x5, waiting for transfers between devices: 21 us -> 0.07 us
    ppermute x0 -> x4, starting transfers between devices: none -> 9.57 us  [_note_panel(): lax.ppermute(low, 'dp', [(j, (j - t1) % value_now) for j in range(value_n...]
    unnamed x47 -> x58, local copies, waits for them, and re-layouts: 1.93 us -> 8.33 us
    reduce_scatter x1, waiting for transfers between devices: 71.4 us -> 74.7 us  [local(): lax.psum_scatter(jnp.concatenate([first, second], axis=1).astype(jnp.bflo...]
  transfers between devices with their start and end apart: 5 -> 8, of which waited for: 4 -> 4; matrix products, arithmetic and copies ran while one was open for 5% -> 5% of each run, Pallas kernels for 0% -> 0%
where the time goes in v1:
time: 250 us; the launch traced here: 249 us
  waiting for transfers between devices  121 us (48%)
  blocking collectives  39.6 us (16%)
  local copies, waits for them, and re-layouts  37.3 us (15%)
  between operations  16 us (6%)
  matrix products  15.8 us (6%)
  starting transfers between devices  9.74 us (4%)
  other arithmetic  9.55 us (4%)
    reduce_scatter x1, waiting for transfers between devices, local(): lax.psum_scatter(jnp.concatenate([first, second], axis=1).astype(jnp.bflo...  74.7 us
    ppermute x4, waiting for transfers between devices, _note_panel(): lax.ppermute(low, 'dp', [(j, (j - t1) % value_now) for j in range(value_n...  46.7 us
    psum x1, blocking collectives, local(): lax.psum(jnp.dot(pooled.T, logit_slope, precision=highest), ('dp', 'vol'))  39.6 us
    gather x1, local copies, waits for them, and re-layouts, render(): picked = jnp.take(table, rows.reshape(-1), axis=0)[:, ::2]  11.4 us
    slice x1, local copies, waits for them, and re-layouts, render(): picked = jnp.take(table, rows.reshape(-1), axis=0)[:, ::2]  10.3 us
    ppermute x4, starting transfers between devices, _note_panel(): lax.ppermute(low, 'dp', [(j, (j - t1) % value_now) for j in range(value_n...  9.57 us
    unnamed x58, local copies, waits for them, and re-layouts  8.33 us
  transfers between devices with their start and end apart: 8, of which 4 were waited for; matrix products, arithmetic and copies ran while one was open for 5% of the time, Pallas kernels for 0%

profile of v1, /device:TPU:0, one launch (start us, length us, event | category | flops | bytes accessed | tf_op | source)
XLA Modules:
  0.0 249.4 jit_solution(2746393875910443105)
XLA Ops:
  8.1 0.7 compare_and_fusion.1
  8.8 0.7 fusion.40
  9.5 11.4 %gather_fusion = bf16[1024,256]{1,0:T(8,128)(2,1)S(1)} fusion(bf16[32768,256]{1,0:T(8,128)(2,1)} %bitcast.104, s32[1024]{0:T(1024)S(1)} %broadcast_clamp_fusion), kind=kCustom, calls=%fused_computation | custom fusion | bytes 1052672 | tf_op jit(solution)/shard_map/jit(_take)/gather | solution.py:80
  21.2 10.3 %slice.21 = bf16[1024,128]{1,0:T(8,128)(2,1)S(1)} slice(bf16[1024,256]{1,0:T(8,128)(2,1)S(1)} %broadcast_select_fusion), slice={[0:1024:1], [0:256:2]} | slice | bytes 524288 | tf_op jit(solution)/shard_map/slice | solution.py:80
  31.7 0.8 convert_element_type.102
  32.5 5.5 %collective-permute-start = (bf16[64,512]{1,0:T(8,128)(2,1)S(1)}, bf16[64,512]{1,0:T(8,128)(2,1)S(1)}, u32[]{:S(2)}, u32[]{:S(2)}) collective-permute-start(bf16[64,512]{1,0:T(8,128)(2,1)S(1)} %copy-done.7), channel_id=1, source_target_pairs={{0,30},{2,0},{4,2},{6,4},{8,6},{10,8},{12,10},{14,12},{16,14},{18,... | collective-permute-start | bytes 196616 | tf_op jit(solution)/shard_map/ppermute | solution.py:22
  38.1 0.5 fusion.21
  38.6 0.5 fusion.23
  39.1 0.6 fusion.26
  39.7 0.6 convert_element_type.105
  41.3 0.6 fusion.9
  42.2 1.1 collective-permute-start.1
  43.3 4.0 %collective-permute-done.1 = bf16[128,512]{1,0:T(8,128)(2,1)S(1)} collective-permute-done((bf16[128,512]{1,0:T(8,128)(2,1)S(1)}, bf16[128,512]{1,0:T(8,128)(2,1)S(1)}, u32[]{:S(2)}, u32[]{:S(2)}) %collective-permute-start.1) | collective-permute-done | bytes 131104 | tf_op jit(solution)/shard_map/ppermute | solution.py:22
  47.3 2.0 collective-permute-start.2
  49.3 0.6 constant_dynamic-update-slice_fusion.9
  49.9 0.6 dynamic-slice
  50.5 0.6 constant_dynamic-update-slice_fusion.8
  51.2 0.7 constant_dynamic-update-slice_fusion.7
  51.8 9.3 %collective-permute-done.2 = bf16[256,512]{1,0:T(8,128)(2,1)S(1)} collective-permute-done((bf16[256,512]{1,0:T(8,128)(2,1)S(1)}, bf16[256,512]{1,0:T(8,128)(2,1)S(1)}, u32[]{:S(2)}, u32[]{:S(2)}) %collective-permute-start.2) | collective-permute-done | bytes 262176 | tf_op jit(solution)/shard_map/ppermute | solution.py:22
  61.1 1.0 collective-permute-start.3
  62.1 1.8 dynamic-slice_convert_fusion
  64.1 0.7 constant_dynamic-update-slice_fusion.6
  64.8 33.5 %collective-permute-done.3 = bf16[512,512]{1,0:T(8,128)(2,1)S(1)} collective-permute-done((bf16[512,512]{1,0:T(8,128)(2,1)S(1)}, bf16[512,512]{1,0:T(8,128)(2,1)S(1)}, u32[]{:S(2)}, u32[]{:S(2)}) %collective-permute-start.3) | collective-permute-done | bytes 524320 | tf_op jit(solution)/shard_map/ppermute | solution.py:22
  98.3 0.8 constant_dynamic-update-slice_fusion.5
  99.1 0.6 constant_dynamic-update-slice_fusion.4
  99.8 0.6 constant_dynamic-update-slice_fusion.3
  100.4 0.7 constant_dynamic-update-slice_fusion.2
  101.1 0.7 constant_dynamic-update-slice_fusion.1
  101.8 0.8 constant_dynamic-update-slice_fusion
  102.6 3.0 %convolution_convert_fusion.1 = bf16[256,1536]{1,0:T(8,128)(2,1)S(1)} fusion(bf16[1024,1536]{1,0:T(8,128)(2,1)} %all-gather.2.cloned.1.call-done, bf16[256,1024]{1,0:T(8,128)(2,1)S(1)} %get-tuple-element.9, f32[1024]{0:T(1024)S(1)} %copy-done.18, f32[256]{0:T(256)S(1)} %add_rsqrt_fusion, f32[256]{0:T(256)S(1)} %broadcast_multiply_fusion.2), kind=kOutput, calls=%fused_computation.5 | convolution fusion | flops 807010304 | bytes 4462592 | tf_op jit(solution)/shard_map/dot_general | solution.py:110
  105.9 0.5 fusion.67
  107.0 1.4 convolution_convert_fusion.5
  109.2 0.8 fusion.68
  110.0 1.2 multiply_reduce_fusion.1
  111.2 1.2 subtract_multiply_fusion
  112.6 1.1 convolution_convert_fusion.4
  113.7 1.5 convolution_convert_fusion.3
  115.2 1.1 copy.34
  116.7 1.5 fusion.4
  118.3 0.6 convolution_bitcast_fusion
  118.9 0.6 convolution_bitcast_fusion.1
  119.6 0.9 copy-done.3
  120.5 1.2 convolution_convert_fusion
  121.7 2.6 %pad_maximum_fusion = bf16[1024,2048]{1,0:T(8,128)(2,1)} fusion(bf16[1024,512]{1,0:T(8,128)(2,1)S(1)} %copy-done.6, bf16[1024,1536]{1,0:T(8,128)(2,1)S(1)} %convolution_convert_fusion), kind=kLoop, calls=%fused_computation.1 | loop fusion | flops 8388608 | bytes 8388608 | tf_op jit(solution)/shard_map/concatenate | solution.py:142
  124.4 74.7 %reduce-scatter.2.cloned.1.call-done = bf16[64,2048]{1,0:T(8,128)(2,1)} async-done(((bf16[1024,2048]{1,0:T(8,128)(2,1)}), bf16[64,2048]{1,0:T(8,128)(2,1)}) %reduce-scatter.2.cloned.1.call-update) | async-done | bytes 262160 | tf_op jit(solution)/shard_map/reduce_scatter | solution.py:141
  199.2 39.6 %psum.15 = f32[1024,4]{0,1:T(4,128)} all-reduce(f32[1024,4]{0,1:T(4,128)S(1)} %broadcast_multiply_fusion), channel_id=1, replica_groups=mesh['dp'=16,'vol'=2] {'dp','vol'}, use_global_device_ids=true, to_apply=%region_11.12 | all-reduce | flops 4096 | bytes 32768 | tf_op jit(solution)/shard_map/psum | solution.py:126
  238.8 1.5 slice.33
  240.3 1.7 slice.32
  (88 shorter events, 4.6 us)
Async XLA Ops:
  8.0 32.9 %copy-start = (bf16[64,1024]{1,0:T(8,128)(2,1)S(1)}, bf16[64,1024]{1,0:T(8,128)(2,1)}, u32[]{:S(2)}) copy-start(bf16[64,1024]{1,0:T(8,128)(2,1)} %param.14) | copy-start | bytes 393220
  8.0 54.1 %all-reduce.9.cloned.1.call-start = ((), (), s32[]{:S(2)}) async-start(), calls=%async_computation.4 | async-start | bytes 524288
  20.9 11.6 %copy-start.7 = (bf16[64,512]{1,0:T(8,128)(2,1)S(1)}, bf16[64,512]{1,0:T(8,128)(2,1)}, u32[]{:S(2)}) copy-start(bf16[64,512]{1,0:T(8,128)(2,1)} %param.18) | copy-start | bytes 196612
  20.9 17.2 %copy-start.9 = (f32[1,128,128]{2,1,0:T(8,128)S(1)}, f32[1,128,128]{2,1,0:T(8,128)}, u32[]{:S(2)}) copy-start(f32[1,128,128]{2,1,0:T(8,128)} %param.10) | copy-start | bytes 196612
  20.9 18.8 %copy-start.10 = (bf16[1,128,128]{2,1,0:T(8,128)(2,1)S(1)}, bf16[1,128,128]{2,1,0:T(8,128)(2,1)}, u32[]{:S(2)}) copy-start(bf16[1,128,128]{2,1,0:T(8,128)(2,1)} %param.11) | copy-start | bytes 98308
  31.4 9.5 %copy-start.8 = (bf16[256,1024]{1,0:T(8,128)(2,1)S(1)}, bf16[256,1024]{1,0:T(8,128)(2,1)}, u32[]{:S(2)}) copy-start(bf16[256,1024]{1,0:T(8,128)(2,1)} %param.15) | copy-start | bytes 1572868
  32.5 70.2 %all-gather.2.cloned.1.call-start = ((), (), s32[]{:S(2)}) async-start(), calls=%async_computation.1 | async-start | bytes 3342336 | tf_op jit(solution)/shard_map/all_gather | solution.py:112
  32.5 9.7 %collective-permute-start = (bf16[64,512]{1,0:T(8,128)(2,1)S(1)}, bf16[64,512]{1,0:T(8,128)(2,1)S(1)}, u32[]{:S(2)}, u32[]{:S(2)}) collective-permute-start(bf16[64,512]{1,0:T(8,128)(2,1)S(1)} %copy-done.7), channel_id=1, source_target_pairs={{0,30},{2,0},{4,2},{6,4},{8,6},{10,8},{12,10},{14,12},{16,14},{18,... | collective-permute-start | bytes 196616 | tf_op jit(solution)/shard_map/ppermute | solution.py:22
  38.0 161.1 %reduce-scatter.2.cloned.1.call-start = ((), (), s32[]{:S(2)}) async-start(), calls=%async_computation.2 | async-start | bytes 4456448 | tf_op jit(solution)/shard_map/reduce_scatter | solution.py:141
  40.3 9.6 %copy-start.23 = (u32[32]{0:T(128)S(1)}, u32[32]{0:T(128)}, u32[]{:S(2)}) copy-start(u32[32]{0:T(128)} %constant.131) | copy-start | bytes 388
  41.3 61.3 %copy-start.1 = (bf16[256,1024]{1,0:T(8,128)(2,1)}, bf16[256,1024]{1,0:T(8,128)(2,1)S(1)}, u32[]{:S(2)}) copy-start(bf16[256,1024]{1,0:T(8,128)(2,1)S(1)} %get-tuple-element.9) | copy-start | bytes 1572868
  41.3 61.3 %copy-start.14 = (f32[256]{0:T(256)}, f32[256]{0:T(256)S(1)}, u32[]{:S(2)}) copy-start(f32[256]{0:T(256)S(1)} %broadcast_multiply_fusion.2) | copy-start | bytes 3076
  42.2 5.0 %collective-permute-start.1 = (bf16[128,512]{1,0:T(8,128)(2,1)S(1)}, bf16[128,512]{1,0:T(8,128)(2,1)S(1)}, u32[]{:S(2)}, u32[]{:S(2)}) collective-permute-start(bf16[128,512]{1,0:T(8,128)(2,1)S(1)} %pad_maximum_fusion.3), channel_id=1, source_target_pairs={{0,28},{2,30},{4,0},{6,2},{8,4},{10,6},{12,8},{14,10},{16,12},{18,... | collective-permute-start | bytes 393224 | tf_op jit(solution)/shard_map/ppermute | solution.py:22
  43.3 59.3 %copy-start.20 = (f32[256]{0:T(256)}, f32[256]{0:T(256)S(1)}, u32[]{:S(2)}) copy-start(f32[256]{0:T(256)S(1)} %add_rsqrt_fusion) | copy-start | bytes 3076
  47.3 13.8 %collective-permute-start.2 = (bf16[256,512]{1,0:T(8,128)(2,1)S(1)}, bf16[256,512]{1,0:T(8,128)(2,1)S(1)}, u32[]{:S(2)}, u32[]{:S(2)}) collective-permute-start(bf16[256,512]{1,0:T(8,128)(2,1)S(1)} %pad_maximum_fusion.2), channel_id=1, source_target_pairs={{0,24},{2,26},{4,28},{6,30},{8,0},{10,2},{12,4},{14,6},{16,8},{18,... | collective-permute-start | bytes 786440 | tf_op jit(solution)/shard_map/ppermute | solution.py:22
  61.1 37.2 %collective-permute-start.3 = (bf16[512,512]{1,0:T(8,128)(2,1)S(1)}, bf16[512,512]{1,0:T(8,128)(2,1)S(1)}, u32[]{:S(2)}, u32[]{:S(2)}) collective-permute-start(bf16[512,512]{1,0:T(8,128)(2,1)S(1)} %pad_maximum_fusion.1), channel_id=1, source_target_pairs={{0,16},{2,18},{4,20},{6,22},{8,24},{10,26},{12,28},{14,30},{16,0},... | collective-permute-start | bytes 1572872 | tf_op jit(solution)/shard_map/ppermute | solution.py:22
  64.0 38.7 %copy-start.18 = (f32[1024]{0:T(1024)S(1)}, f32[1024]{0:T(1024)}, u32[]{:S(2)}) copy-start(f32[1024]{0:T(1024)} %param.16) | copy-start | bytes 12292
  105.9 0.9 copy-start.4
  106.8 1.6 copy-start.2
  106.8 1.8 copy-start.22
  107.0 2.2 copy-start.11
  109.2 4.5 %copy-start.12 = (f32[1024]{0:T(1024)}, f32[1024]{0:T(1024)S(1)}, u32[]{:S(2)}) copy-start(f32[1024]{0:T(1024)S(1)} %broadcast_multiply_fusion.1) | copy-start | bytes 12292
  112.4 1.3 copy-start.16
  116.7 1.6 copy-start.5
  119.5 1.0 copy-start.3
  119.5 1.0 copy-start.15
  119.5 1.0 copy-start.19
  119.5 1.0 copy-start.21
  120.5 1.2 copy-start.6
  124.3 74.8 %copy-start.13 = (f32[1024]{0:T(1024)S(1)}, f32[1024]{0:T(1024)}, u32[]{:S(2)}) copy-start(f32[1024]{0:T(1024)} %copy-done.12) | copy-start | bytes 12292
  124.3 74.8 %copy-start.17 = (f32[4]{0:T(128)S(1)}, f32[4]{0:T(128)}, u32[]{:S(2)}) copy-start(f32[4]{0:T(128)} %copy-done.16) | copy-start | bytes 52
  124.4 114.4 %all-reduce.7.cloned.1.call-start = ((), (), s32[]{:S(2)}) async-start(), calls=%async_computation.3 | async-start | bytes 524288 | tf_op jit(solution)/shard_map/psum | solution.py:147
Sparse Core Ops, SparseCore 0:
  32.6 25.9 all-reduce.8
  199.2 22.3 all-reduce.6
Sparse Core Ops, SparseCore 1:
  38.1 57.0 all-gather.1
  124.5 74.6 reduce-scatter.1
